TPU v7x, 256 devices: a whole 4x4x8 slice. The times are simulated.
256 devices in a mesh: ctx: 32 (over y, z), head: 8 (over x, core).
Axes of the slice: x: 4, y: 4, z: 8, core: 2. Of those that a mesh axis runs over, the one named last changes fastest.
Arguments:
- queries: bfloat16 [32768, 4096], P('ctx', 'head'), as said below
- key_value: bfloat16 [2, 32768, 4096], P(None, 'ctx', 'head'), as said below
- lanczos_vec: float32 [32768, 4096], P('ctx', 'head'), as said below
- rand_blocks: int32 [256, 3], replicated, may hold values from 0 to 255, as said below
- global_ids: int32 [2], replicated, may hold values from 0 to 255
Outputs:
- next_vec: float32 [32768, 4096], P('ctx', 'head')
- coefficients: float32 [2], replicated
Inputs may be any that keep to these rules, and one draw needn't show every extreme that they name: `rand_blocks`: row b lists the random key blocks of query block b. For each shard of 8 query blocks along ctx and each shard of 8 key blocks, at most 1 of the shard's listed random blocks lie in that key shard, and every query shard reaches 1 with some key shard. `queries`: entries are of order one or a few tens. `key_value`: keys of order one, values of order one to a few hundred. `lanczos_vec`: nonzero real entries; the mean of their squares over all entries is one, up to float32 rounding.
All inputs are finite; a program needn't handle non-finite values.
Results may differ from a plain program's by a relative error of at most 0.0049.
Values may be sent and summed in bfloat16 or wider, within the bound.
No kernel may reach another device: no remote copies, remote signals or barrier semaphores. Data moves between devices by JAX's collectives and lax.ppermute only.
A program may use at most 128 MiB of HBM per device.

v0:
```python
import jax
import jax.numpy as jnp
from jax import lax
from jax.sharding import PartitionSpec as P

HD = 128
BS = 128


def padded_2(cells, sides, width):
    for axis, dim in sides:
        count = lax.axis_size(axis)
        ends = count - 1
        head = lax.slice_in_dim(cells, 0, width, axis=dim)
        tail = lax.slice_in_dim(cells, cells.shape[dim] - width, cells.shape[dim], axis=dim)
        cells = jnp.concatenate(
            [
                lax.ppermute(tail, axis, [(i, (i + 1) % count) for i in range(ends)]),
                cells,
                lax.ppermute(head, axis, [((i + 1) % count, i) for i in range(ends)]),
            ],
            axis=dim,
        )
    return cells


def from_root(block, axis, holder):
    block = jnp.where(lax.axis_index(axis) == holder, block, jnp.zeros_like(block))
    return lax.psum(block, axis)


def local(queries, key_value, lanczos_vec, rand_blocks, global_ids):
    tok_rows = queries.shape[0]
    col_width = queries.shape[1]
    nblocks = tok_rows // BS
    local_heads = col_width // HD
    ctx_count = lax.axis_size("ctx")
    ctx_index = lax.axis_index("ctx")
    random_count = rand_blocks.shape[1]
    glob_count = global_ids.shape[0]
    capacity = (nblocks * random_count + ctx_count - 1) // ctx_count
    score_scale = HD ** (-0.5)
    blocks_kv = key_value.reshape(2, nblocks, BS, col_width)
    padded = padded_2(key_value, (("ctx", 1),), BS)
    window = jnp.concatenate(
        [
            padded[:, offset * BS : offset * BS + tok_rows].reshape(2, nblocks, BS, col_width)
            for offset in range(3)
        ],
        axis=2,
    )
    owners = global_ids // nblocks
    places = global_ids % nblocks
    requests = rand_blocks.reshape(ctx_count, nblocks * random_count)
    sources = requests // nblocks
    inside = requests % nblocks
    is_mine = (sources == ctx_index).astype(jnp.int32)
    earlier = jnp.cumsum(is_mine, axis=1) - is_mine
    slot_ids = jnp.arange(capacity, dtype=jnp.int32)
    matched = (is_mine[:, :, None] == 1) & (earlier[:, :, None] == slot_ids[None, None, :])
    chosen = jnp.sum(jnp.where(matched, inside[:, :, None], 0), axis=1)
    outgoing = jnp.take(blocks_kv, chosen.reshape(-1), axis=1)
    own_list = lax.dynamic_index_in_dim(requests, ctx_index, 0, keepdims=False)
    own_sources = own_list // nblocks
    request_total = own_list.shape[0]
    before_mask = jnp.arange(request_total)[:, None] > jnp.arange(request_total)[None, :]
    same_source = own_sources[:, None] == own_sources[None, :]
    order_rank = jnp.sum((before_mask & same_source).astype(jnp.int32), axis=1)
    pieces = []
    for global_pos in range(glob_count):
        block_piece = lax.dynamic_slice_in_dim(key_value, places[global_pos] * BS, BS, 1)
        pieces.append(from_root(block_piece, "ctx", owners[global_pos]))
    global_kv = jnp.concatenate(pieces, axis=1)
    incoming = lax.all_to_all(outgoing, "ctx", split_axis=1, concat_axis=1, tiled=True)
    random_kv = jnp.take(incoming, own_sources * capacity + order_rank, axis=1)
    random_kv = random_kv.reshape(2, nblocks, random_count * BS, col_width)
    global_wide = jnp.broadcast_to(global_kv[:, None], (2, nblocks, glob_count * BS, col_width))
    listed_kv = jnp.concatenate([window, global_wide, random_kv], axis=2)
    key_total = listed_kv.shape[2]
    key_position = jnp.arange(key_total)[None, :]
    block_index = jnp.arange(nblocks)[:, None]
    left_bad = (block_index == 0) & (key_position < BS) & (ctx_index == 0)
    right_bad = (
        (block_index == nblocks - 1)
        & (key_position >= 2 * BS)
        & (key_position < 3 * BS)
        & (ctx_index == ctx_count - 1)
    )
    valid_keys = jnp.logical_not(left_bad | right_bad)
    group_size = min(nblocks, max(1, 512 // BS))
    group_count = nblocks // group_size
    query_groups = queries.reshape(group_count, group_size, BS, local_heads, HD)
    tangent_groups = lanczos_vec.astype(jnp.bfloat16).reshape(
        group_count, group_size, BS, local_heads, HD
    )
    key_groups = listed_kv[0].reshape(group_count, group_size, key_total, local_heads, HD)
    value_groups = listed_kv[1].reshape(group_count, group_size, key_total, local_heads, HD)
    valid_groups = valid_keys.reshape(group_count, group_size, key_total)

    def attend(inputs_group):
        query_part, tangent, key_part, values, valid_part = inputs_group
        valid_wide = valid_part[:, None, None, :]
        scores = (
            jnp.einsum("bqhd,bkhd->bhqk", query_part, key_part, preferred_element_type=jnp.float32)
            * score_scale
        )
        row_top = jnp.max(jnp.where(valid_wide, scores, -jnp.inf), axis=-1, keepdims=True)
        weights = jnp.where(valid_wide, jnp.exp(scores - row_top), 0.0)
        attention = weights / jnp.sum(weights, axis=-1, keepdims=True)
        dscore = (
            jnp.einsum("bqhd,bkhd->bhqk", tangent, key_part, preferred_element_type=jnp.float32)
            * score_scale
        )
        center = jnp.sum(attention * dscore, axis=-1, keepdims=True)
        first_grad = (attention * (dscore - center)).astype(jnp.bfloat16)
        tangent_out = jnp.einsum(
            "bhqk,bkhd->bqhd", first_grad, values, preferred_element_type=jnp.float32
        ).astype(jnp.bfloat16)
        back_prob = jnp.einsum(
            "bqhd,bkhd->bhqk", tangent_out, values, preferred_element_type=jnp.float32
        )
        center_two = jnp.sum(attention * back_prob, axis=-1, keepdims=True)
        second_grad = (attention * (back_prob - center_two)).astype(jnp.bfloat16)
        return (
            jnp.einsum("bhqk,bkhd->bqhd", second_grad, key_part, preferred_element_type=jnp.float32)
            * score_scale
        )

    product = lax.map(
        attend, (query_groups, tangent_groups, key_groups, value_groups, valid_groups)
    )
    product = product.reshape(tok_rows, col_width)
    entry_count = float(tok_rows * col_width * ctx_count * lax.axis_size("head"))
    alpha_coef = lax.psum(jnp.sum(lanczos_vec * product), ("ctx", "head")) / entry_count
    residual = product - alpha_coef * lanczos_vec
    square_sum = lax.psum(jnp.sum(residual * residual), ("ctx", "head"))
    beta_coef = jnp.sqrt(square_sum / entry_count + 1e-06)
    coefficients = jnp.stack([alpha_coef, beta_coef])
    return (residual / beta_coef, coefficients)


def solution(mesh):
    placed = (P("ctx", "head"), P(None, "ctx", "head"), P("ctx", "head"), P(), P())
    return jax.shard_map(
        local, mesh=mesh, in_specs=placed, out_specs=(P("ctx", "head"), P()), check_vma=False
    )
```

profile of v0, /device:TPU:1, one launch (start us, length us, event | category | flops | bytes accessed | tf_op | source)
XLA Modules:
  0.0 574.3 jit_solution(9242405186403355170)
XLA Ops:
  9.8 6.5 %gather_fusion = bf16[32,2,128,512]{3,2,1,0:T(8,128)(2,1)} fusion(bf16[2,8,128,512]{3,2,1,0:T(8,128)(2,1)} %bitcast.136, s32[1024]{0:T(1024)S(1)} %pad_clamp_fusion.1), kind=kCustom, calls=%fused_computation | custom fusion | bytes 16777344 | tf_op jit(solution)/shard_map/jit(_take)/gather | solution.py:62
  16.3 7.5 %select_bitcast_fusion = bf16[2,32,128,512]{3,2,0,1:T(8,128)(2,1)} fusion(bf16[32,2,128,512]{3,2,1,0:T(8,128)(2,1)} %gather_fusion, pred[32]{0:T(512)(128)(4,1)S(1)} %compare_and_fusion), kind=kLoop, calls=%fused_computation.51 | loop fusion | flops 4194304 | bytes 16777248 | tf_op jit(solution)/shard_map/jit(_take)/select_n | solution.py:62
  23.8 12.3 %all-to-all-start = ((bf16[2,32,128,512]{3,2,0,1:T(8,128)(2,1)}), bf16[2,32,128,512]{3,2,0,1:T(8,128)(2,1)}, u32[]{:S(2)}, u32[]{:S(2)}) async-start(bf16[2,32,128,512]{3,2,0,1:T(8,128)(2,1)} %select_bitcast_fusion), calls=%async_computation | async-start | bytes 16777216 | tf_op jit(solution)/shard_map/all_to_all | solution.py:74
  40.3 3.7 collective-permute-start
  52.3 179.7 %collective-permute-done = bf16[2,128,512]{2,1,0:T(8,128)(2,1)} collective-permute-done((bf16[2,128,512]{2,1,0:T(8,128)(2,1)}, bf16[2,128,512]{2,1,0:T(8,128)(2,1)}, u32[]{:S(2)}, u32[]{:S(2)}) %collective-permute-start) | collective-permute-done | bytes 262176 | tf_op jit(solution)/shard_map/ppermute | solution.py:18
  237.9 23.7 %all-reduce.3.cloned.1.call-done = (bf16[2,128,512]{2,1,0:T(8,128)(2,1)}, bf16[2,128,512]{2,1,0:T(8,128)(2,1)}) async-done(((bf16[2,128,512]{2,1,0:T(8,128)(2,1)}, bf16[2,128,512]{2,1,0:T(8,128)(2,1)}), (bf16[2,128,512]{2,1,0:T(8,128)(2,1)}, bf16[2,128,512]{2,1,0:T(8,128)(2,1)})) %all-reduce.3.cloned.1.call-update) | async-done | bytes 524304 | tf_op jit(solution)/shard_map/psum | solution.py:29
  265.0 7.9 %gather_fusion.1 = bf16[24,2,128,512]{3,2,1,0:T(8,128)(2,1)} fusion(bf16[2,32,128,512]{3,2,0,1:T(8,128)(2,1)} %all-to-all-done, s32[1024]{0:T(1024)S(1)} %pad_clamp_fusion), kind=kCustom, calls=%fused_computation.1 | custom fusion | bytes 12583008 | tf_op jit(solution)/shard_map/jit(_take)/gather | solution.py:75
  272.9 3.5 copy.63
  279.9 11.3 %fusion.74 = (bf16[1,8,1024,512]{3,2,1,0:T(8,128)(2,1)}, bf16[1,8,1024,512]{3,2,1,0:T(8,128)(2,1)}) fusion(bf16[2,8,1024,512]{3,2,1,0:T(8,128)(2,1)} %fusion.48), kind=kLoop, calls=%fused_computation.147 | loop fusion | bytes 33554432 | tf_op jit(solution)/shard_map/slice | solution.py:97
  291.2 11.5 %copy.64 = bf16[1,8,1024,512]{2,3,1,0:T(8,128)(2,1)} copy(bf16[1,8,1024,512]{3,2,1,0:T(8,128)(2,1)} %get-tuple-element.88) | data formatting | bytes 16777216 | tf_op jit(solution)/shard_map/slice | solution.py:96
  302.6 11.4 %copy.65 = bf16[1,8,1024,512]{2,3,1,0:T(8,128)(2,1)} copy(bf16[1,8,1024,512]{3,2,1,0:T(8,128)(2,1)} %get-tuple-element.87) | data formatting | bytes 16777216 | tf_op jit(solution)/shard_map/slice | solution.py:97
  314.0 90.9 %while.10 = (s32[]{:T(128)}, f32[2,4,128,4,128]{4,3,2,1,0:T(4,128)}, bf16[2,4,1024,4,128]{2,4,3,1,0:T(8,128)(2,1)}, pred[2,4,1024]{2,1,0:T(4,128)(4,1)S(1)}, bf1...) while((s32[]{:T(128)}, ...), condition=%wide.region_11.12_spmd, body=%wide.region_6.11_spmd.sunk | while | flops 2731013120 | bytes 146889360 | solution.py:129
  315.8 3.6 fusion.86
  319.4 4.7 fusion.87
  324.2 6.5 %multiply_reduce_fusion.5 = (f32[4,4,128]{2,1,0:T(4,128)S(1)}, f32[4,4,128,1024]{3,2,1,0:T(8,128)}) fusion(f32[4,4,128,1024]{3,2,1,0:T(8,128)} %get-tuple-element.159, f32[4,4,128]{2,1,0:T(4,128)S(1)} %get-tuple-element.160, bf16[2,4,1024,4,128]{2,4,3,1,0:T(8,128)(2,1)S(1)} %bitcast.135, s32[]{:T(128)} %get-tuple-element.174, ...), kind=kOutput, calls=%fused_computation.6.clone.1 | convolution fusion | flops 545257472 | bytes 21512196 | tf_op jit(solution)/shard_map/while/body/eval_jaxpr/bqhd,bkhd->bhqk/dot_general | solution.py:111
  330.6 16.5 %multiply_reduce_fusion.6 = (f32[4,4,128]{2,1,0:T(4,128)S(1)}, f32[4,4,128,1024]{3,2,1,0:T(8,128)}) fusion(f32[4,4,128,1024]{3,2,1,0:T(8,128)} %get-tuple-element.159, f32[4,4,128]{2,1,0:T(4,128)S(1)} %get-tuple-element.160, bf16[2,4,1024,4,128]{2,4,3,1,0:T(8,128)(2,1)} %get-tuple-element.187, s32[]{:T(128)} %get-tuple-element.174, ...), kind=kOutput, calls=%fused_computation.4.clone.1 | convolution fusion | flops 1090779136 | bytes 41976832 | tf_op jit(solution)/shard_map/while/body/eval_jaxpr/bqhd,bkhd->bhqk/dot_general | solution.py:119
  347.1 9.8 %fusion.88 = f32[1,4,128,4,128]{2,4,3,1,0:T(8,128)} fusion(f32[4,4,128,1024]{3,2,1,0:T(8,128)} %get-tuple-element.164, f32[4,4,128]{2,1,0:T(4,128)S(1)} %get-tuple-element.165, bf16[2,4,1024,4,128]{2,4,3,1,0:T(8,128)(2,1)} %get-tuple-element.184, s32[]{:T(128)} %get-tuple-element.174, f32[4,4,128,1024]{3,2,1,0:T(8,128)} %get-tuple-element.159, ...), kind=kOutput, calls=%fused_computation.34.clone.1 | convolution fusion | flops 545521664 | bytes 22036992 | tf_op jit(solution)/shard_map/while/body/eval_jaxpr/bhqk,bkhd->bqhd/dot_general | solution.py:125
  361.2 3.6 fusion.86
  364.8 4.7 fusion.87
  369.6 6.5 %multiply_reduce_fusion.5 = (f32[4,4,128]{2,1,0:T(4,128)S(1)}, f32[4,4,128,1024]{3,2,1,0:T(8,128)}) fusion(f32[4,4,128,1024]{3,2,1,0:T(8,128)} %get-tuple-element.159, f32[4,4,128]{2,1,0:T(4,128)S(1)} %get-tuple-element.160, bf16[2,4,1024,4,128]{2,4,3,1,0:T(8,128)(2,1)S(1)} %bitcast.135, s32[]{:T(128)} %get-tuple-element.174, ...), kind=kOutput, calls=%fused_computation.6.clone.1 | convolution fusion | flops 545257472 | bytes 21512196 | tf_op jit(solution)/shard_map/while/body/eval_jaxpr/bqhd,bkhd->bhqk/dot_general | solution.py:111
  376.0 16.3 %multiply_reduce_fusion.6 = (f32[4,4,128]{2,1,0:T(4,128)S(1)}, f32[4,4,128,1024]{3,2,1,0:T(8,128)}) fusion(f32[4,4,128,1024]{3,2,1,0:T(8,128)} %get-tuple-element.159, f32[4,4,128]{2,1,0:T(4,128)S(1)} %get-tuple-element.160, bf16[2,4,1024,4,128]{2,4,3,1,0:T(8,128)(2,1)} %get-tuple-element.187, s32[]{:T(128)} %get-tuple-element.174, ...), kind=kOutput, calls=%fused_computation.4.clone.1 | convolution fusion | flops 1090779136 | bytes 41976832 | tf_op jit(solution)/shard_map/while/body/eval_jaxpr/bqhd,bkhd->bhqk/dot_general | solution.py:119
  392.4 9.8 %fusion.88 = f32[1,4,128,4,128]{2,4,3,1,0:T(8,128)} fusion(f32[4,4,128,1024]{3,2,1,0:T(8,128)} %get-tuple-element.164, f32[4,4,128]{2,1,0:T(4,128)S(1)} %get-tuple-element.165, bf16[2,4,1024,4,128]{2,4,3,1,0:T(8,128)(2,1)} %get-tuple-element.184, s32[]{:T(128)} %get-tuple-element.174, f32[4,4,128,1024]{3,2,1,0:T(8,128)} %get-tuple-element.159, ...), kind=kOutput, calls=%fused_computation.34.clone.1 | convolution fusion | flops 545521664 | bytes 22036992 | tf_op jit(solution)/shard_map/while/body/eval_jaxpr/bhqk,bkhd->bqhd/dot_general | solution.py:125
  407.7 79.1 %psum.30 = f32[]{:T(128)} all-reduce(f32[]{:T(128)} %fusion.49), channel_id=1, replica_groups=mesh['ctx'=32,'head'=8] {'ctx','head'}, use_global_device_ids=true, to_apply=%region_13.14 | all-reduce | flops 1 | bytes 8 | tf_op jit(solution)/shard_map/psum | solution.py:134
  490.2 72.6 %psum.31 = f32[]{:T(128)} all-reduce(f32[]{:T(128)} %multiply_reduce_fusion.2), channel_id=1, replica_groups=mesh['ctx'=32,'head'=8] {'ctx','head'}, use_global_device_ids=true, to_apply=%region_15.16 | all-reduce | flops 1 | bytes 8 | tf_op jit(solution)/shard_map/psum | solution.py:136
  (77 shorter events, 43.3 us)
Async XLA Ops:
  23.8 12.4 %copy-start.2 = (s32[2]{0:T(128)S(1)}, s32[2]{0:T(128)}, u32[]{:S(2)}) copy-start(s32[2]{0:T(128)} %param.11) | copy-start | bytes 28
  23.8 15.6 %copy-start = (bf16[2,1024,512]{2,1,0:T(8,128)(2,1)S(1)}, bf16[2,1024,512]{2,1,0:T(8,128)(2,1)}, u32[]{:S(2)}) copy-start(bf16[2,1024,512]{2,1,0:T(8,128)(2,1)} %param.8) | copy-start | bytes 6291460
  23.8 241.2 %all-to-all-start = ((bf16[2,32,128,512]{3,2,0,1:T(8,128)(2,1)}), bf16[2,32,128,512]{3,2,0,1:T(8,128)(2,1)}, u32[]{:S(2)}, u32[]{:S(2)}) async-start(bf16[2,32,128,512]{3,2,0,1:T(8,128)(2,1)} %select_bitcast_fusion), calls=%async_computation | async-start | bytes 16777216 | tf_op jit(solution)/shard_map/all_to_all | solution.py:74
  36.1 225.5 %all-reduce.3.cloned.1.call-start = ((), (), s32[]{:S(2)}) async-start(), calls=%async_computation.1 | async-start | bytes 1048576 | tf_op jit(solution)/shard_map/psum | solution.py:29
  40.3 191.7 %collective-permute-start = (bf16[2,128,512]{2,1,0:T(8,128)(2,1)}, bf16[2,128,512]{2,1,0:T(8,128)(2,1)}, u32[]{:S(2)}, u32[]{:S(2)}) collective-permute-start(bf16[2,128,512]{2,1,0:T(8,128)(2,1)} %get-tuple-element.91), channel_id=1, source_target_pairs={{0,8},{8,16},{16,24},{24,32},{32,40},{40,48},{48,56},{56,64},{64,7... | collective-permute-start | bytes 786440 | tf_op jit(solution)/shard_map/ppermute | solution.py:18
  44.1 188.0 %collective-permute-start.1 = (bf16[2,128,512]{2,1,0:T(8,128)(2,1)S(1)}, bf16[2,128,512]{2,1,0:T(8,128)(2,1)}, u32[]{:S(2)}, u32[]{:S(2)}) collective-permute-start(bf16[2,128,512]{2,1,0:T(8,128)(2,1)S(1)} %get-tuple-element.90), channel_id=1, source_target_pairs={{8,0},{16,8},{24,16},{32,24},{40,32},{48,40},{56,48},{64,56},{72,6... | collective-permute-start | bytes 786440 | tf_op jit(solution)/shard_map/ppermute | solution.py:20
  314.0 90.9 %copy-start.1 = (f32[1024,512]{1,0:T(8,128)S(1)}, f32[1024,512]{1,0:T(8,128)}, u32[]{:S(2)}) copy-start(f32[1024,512]{1,0:T(8,128)} %param.9) | copy-start | bytes 6291460
  315.8 8.4 %slice-start = ((s8[8388608]{0:T(1024)(128)(4,1)}), s8[4194304]{0:T(1024)(128)(4,1)S(1)}, s32[]{:S(2)}) async-start(s8[8388608]{0:T(1024)(128)(4,1)} %bitcast.134), calls=%async_computation.2 | async-start | bytes 8388608 | tf_op jit(solution)/shard_map/while
  319.4 4.8 slice-start.1
  361.2 8.4 %slice-start = ((s8[8388608]{0:T(1024)(128)(4,1)}), s8[4194304]{0:T(1024)(128)(4,1)S(1)}, s32[]{:S(2)}) async-start(s8[8388608]{0:T(1024)(128)(4,1)} %bitcast.134), calls=%async_computation.2 | async-start | bytes 8388608 | tf_op jit(solution)/shard_map/while
  364.8 4.8 slice-start.1
Sparse Core Ops, SparseCore 0:
  45.5 216.0 all-reduce.2
where the time goes:
time: 576 us; the launch traced here: 574 us
  waiting for transfers between devices  203 us (35%)
  blocking collectives  152 us (26%)
  local copies, waits for them, and re-layouts  74.4 us (13%)
  matrix products  72.6 us (13%)
  other arithmetic  36.6 us (6%)
  between operations  18.1 us (3%)
  starting transfers between devices  17.4 us (3%)
    ppermute x1, waiting for transfers between devices, padded_2(): lax.ppermute(tail, axis, [(i, (i + 1) % count) for i in range(ends)])  180 us
    psum x1, blocking collectives, local(): lax.psum(jnp.sum(lanczos_vec * product), ('ctx', 'head')) / entry_count  79.1 us
    psum x1, blocking collectives, local(): square_sum = lax.psum(jnp.sum(residual * residual), ('ctx', 'head'))  72.6 us
    dot_general x2, matrix products, attend(): jnp.einsum('bqhd,bkhd->bhqk', tangent_out, values, preferred_element_type...  32.8 us
    psum x1, waiting for transfers between devices, from_root(): return lax.psum(block, axis)  23.7 us
    slice x2, local copies, waits for them, and re-layouts, local(): listed_kv[1].reshape(group_count, group_size, key_total, local_heads, HD)  22.7 us
    dot_general x2, matrix products, attend(): jnp.einsum('bhqk,bkhd->bqhd', second_grad, key_part, preferred_element_ty...  19.7 us
    dot_general x2, matrix products, attend(): jnp.einsum('bqhd,bkhd->bhqk', tangent, key_part, preferred_element_type=j...  12.9 us
  transfers between devices with their start and end apart: 4, of which 2 were waited for; matrix products, arithmetic and copies ran while one was open for 3% of the time, Pallas kernels for 0%

commit v1 on v0

v1 whole, which is shorter than its diff:
```python
import functools

import jax
import jax.numpy as jnp
from jax import lax
from jax.experimental import pallas as pl
from jax.experimental.pallas import tpu as pltpu
from jax.sharding import PartitionSpec as P

HD = 128
BS = 128
LIST = 8
SCALE = HD ** (-0.5)
LOG2E = 1.4426950408889634
NT = (((1,), (1,)), ((), ()))


def attend_tile(q, tangent, keys, values, left_bias, right_bias):
    both = jnp.concatenate([q, tangent], axis=0)
    logits = lax.dot_general(both, keys, NT, preferred_element_type=jnp.float32)
    scores = logits[:BS]
    dots = logits[BS:]
    scores = jnp.concatenate(
        [
            scores[:, :BS] + left_bias,
            scores[:, BS : 2 * BS],
            scores[:, 2 * BS : 3 * BS] + right_bias,
            scores[:, 3 * BS :],
        ],
        axis=1,
    )
    row_top = jnp.max(scores, axis=1, keepdims=True)
    weights = jnp.exp2((scores - row_top) * (SCALE * LOG2E))
    inv_total = 1.0 / jnp.sum(weights, axis=1, keepdims=True)
    prob = weights * inv_total
    center = jnp.sum(prob * dots, axis=1, keepdims=True)
    first = ((prob * SCALE) * (dots - center)).astype(jnp.bfloat16)
    dout = jnp.dot(first, values, preferred_element_type=jnp.float32).astype(jnp.bfloat16)
    dprob = lax.dot_general(dout, values, NT, preferred_element_type=jnp.float32)
    center_two = jnp.sum(prob * dprob, axis=1, keepdims=True)
    second = (prob * (dprob - center_two)).astype(jnp.bfloat16)
    return jnp.dot(second, keys, preferred_element_type=jnp.float32) * SCALE


def attention_kernel(
    nblocks, rand_ref, edge_ref, q_ref, vec_ref, own, left, right, glob, rand,
    out_ref, stat_ref, kbuf, vbuf, sems, acc,
):
    b = pl.program_id(0)
    width = q_ref.shape[1]

    def copies(blk, slot, start):
        def move(src, pos):
            for kv, buf in enumerate((kbuf, vbuf)):
                cp = pltpu.make_async_copy(
                    src(kv), buf.at[slot, pl.ds(pos * BS, BS)], sems.at[slot, kv, pos]
                )
                if start:
                    cp.start()
                else:
                    cp.wait()

        if start:
            @pl.when(blk == 0)
            def _():
                move(lambda kv: left.at[kv], 0)

            @pl.when(blk > 0)
            def _():
                move(lambda kv: own.at[kv, blk - 1], 0)

            @pl.when(blk == nblocks - 1)
            def _():
                move(lambda kv: right.at[kv], 2)

            @pl.when(blk < nblocks - 1)
            def _():
                move(lambda kv: own.at[kv, blk + 1], 2)
        else:
            move(lambda kv: left.at[kv], 0)
            move(lambda kv: left.at[kv], 2)
        move(lambda kv: own.at[kv, blk], 1)
        for g in range(2):
            move(lambda kv: glob.at[kv, g], 3 + g)
        for r in range(3):
            move(lambda kv: rand.at[kv, rand_ref[blk * 3 + r]], 5 + r)

    slot = lax.rem(b, 2)

    @pl.when(b == 0)
    def _():
        copies(0, 0, True)

    @pl.when(b + 1 < nblocks)
    def _():
        copies(b + 1, 1 - slot, True)

    copies(b, slot, False)
    left_bias = jnp.where((b == 0) & (edge_ref[0] == 1), -1e30, 0.0).astype(jnp.float32)
    right_bias = jnp.where((b == nblocks - 1) & (edge_ref[1] == 1), -1e30, 0.0).astype(jnp.float32)
    for h in range(width // HD):
        cols = slice(h * HD, (h + 1) * HD)
        vec = vec_ref[:, cols]
        prod = attend_tile(
            q_ref[:, cols], vec.astype(jnp.bfloat16), kbuf[slot, :, cols], vbuf[slot, :, cols],
            left_bias, right_bias,
        )
        out_ref[:, cols] = prod
        s = jnp.sum(vec * vec, axis=0, keepdims=True)
        c = jnp.sum(vec * prod, axis=0, keepdims=True)
        a = jnp.where(s > 0, c / jnp.where(s > 0, s, 1.0), 0.0)
        d = prod - a * vec
        acc[b, 0:1, cols] = s
        acc[b, 1:2, cols] = c
        acc[b, 2:3, cols] = jnp.sum(d * d, axis=0, keepdims=True)

    @pl.when(b == nblocks - 1)
    def _():
        s, c, r = combine(acc[:, 0, :], acc[:, 1, :], acc[:, 2, :])
        lane = lax.broadcasted_iota(jnp.int32, stat_ref.shape, 1)
        stat_ref[...] = jnp.where(lane == 0, s, jnp.where(lane == 1, c, jnp.where(lane == 2, r, 0.0)))


def total(x):
    return jnp.sum(jnp.sum(x, axis=0, keepdims=True), axis=1, keepdims=True)


def combine(s, c, r):
    s_all = total(s)
    c_all = total(c)
    a = jnp.where(s > 0, c / jnp.where(s > 0, s, 1.0), 0.0)
    a_all = jnp.where(s_all > 0, c_all / jnp.where(s_all > 0, s_all, 1.0), 0.0)
    gap = a - a_all
    return s_all, c_all, total(r + (s * gap) * gap)


def finish_kernel(count, gathered, prod_ref, vec_ref, out_ref, coef_ref, ab):
    @pl.when(pl.program_id(0) == 0)
    def _():
        table = gathered[...]
        s, c, r = table[:, 0:1], table[:, 1:2], table[:, 2:3]
        alpha = total(c) * (1.0 / count)
        slope = jnp.where(s > 0, c / jnp.where(s > 0, s, 1.0), 0.0)
        gap = slope - alpha
        square = total(r + (s * gap) * gap)
        beta = jnp.sqrt(square * (1.0 / count) + 1e-06)
        ab[0:1, :] = jnp.broadcast_to(alpha, (1, 128))
        ab[1:2, :] = jnp.broadcast_to(1.0 / beta, (1, 128))
        lane = lax.broadcasted_iota(jnp.int32, coef_ref.shape, 1)
        coef_ref[...] = jnp.where(lane == 0, alpha, beta)

    alpha = ab[0:1, 0:1]
    inv = ab[1:2, 0:1]
    out_ref[...] = (prod_ref[...] - alpha * vec_ref[...]) * inv


def from_root(block, axis, holder):
    block = jnp.where(lax.axis_index(axis) == holder, block, jnp.zeros_like(block))
    return lax.psum(block, axis)


def local(queries, key_value, lanczos_vec, rand_blocks, global_ids):
    rows, width = queries.shape
    nblocks = rows // BS
    nctx = lax.axis_size("ctx")
    nhead = lax.axis_size("head")
    me = lax.axis_index("ctx")
    own = key_value.reshape(2, nblocks, BS, width)
    left = lax.ppermute(own[:, nblocks - 1], "ctx", [(i, i + 1) for i in range(nctx - 1)])
    right = lax.ppermute(own[:, 0], "ctx", [(i + 1, i) for i in range(nctx - 1)])
    glob = jnp.stack(
        [
            from_root(
                lax.dynamic_index_in_dim(own, global_ids[g] % nblocks, 1, keepdims=False),
                "ctx", global_ids[g] // nblocks,
            )
            for g in range(2)
        ],
        axis=1,
    )
    requests = rand_blocks.reshape(nctx, nblocks * 3)
    mine = requests // nblocks == me
    chosen = jnp.sum(jnp.where(mine, requests % nblocks, 0), axis=1)
    outgoing = jnp.take(own, chosen, axis=1)
    incoming = lax.all_to_all(outgoing, "ctx", split_axis=1, concat_axis=1, tiled=True)
    rand_slots = lax.dynamic_index_in_dim(requests, me, 0, keepdims=False) // nblocks
    edges = jnp.stack([(me == 0).astype(jnp.int32), (me == nctx - 1).astype(jnp.int32)])
    any_spec = pl.BlockSpec(memory_space=pl.ANY)
    row_spec = pl.BlockSpec((BS, width), lambda b, *_: (b, 0))
    product, stats = pl.pallas_call(
        functools.partial(attention_kernel, nblocks),
        out_shape=(
            jax.ShapeDtypeStruct((rows, width), jnp.float32),
            jax.ShapeDtypeStruct((8, 128), jnp.float32),
        ),
        grid_spec=pltpu.PrefetchScalarGridSpec(
            num_scalar_prefetch=2,
            grid=(nblocks,),
            in_specs=[row_spec, row_spec] + [any_spec] * 5,
            out_specs=(row_spec, pl.BlockSpec((8, 128), lambda b, *_: (0, 0))),
            scratch_shapes=[
                pltpu.VMEM((2, LIST * BS, width), jnp.bfloat16),
                pltpu.VMEM((2, LIST * BS, width), jnp.bfloat16),
                pltpu.SemaphoreType.DMA((2, 2, LIST)),
                pltpu.VMEM((nblocks, 8, width), jnp.float32),
            ],
        ),
        name="attend",
    )(rand_slots, edges, queries, lanczos_vec, own, left, right, glob, incoming)
    sent = jnp.broadcast_to(stats[:1], (nctx * nhead, 128))
    gathered = lax.all_to_all(sent, ("ctx", "head"), 0, 0, tiled=True)
    count = float(rows * width * nctx * nhead)
    step = rows // 4
    fin_spec = pl.BlockSpec((step, width), lambda i: (i, 0))
    next_vec, coef = pl.pallas_call(
        functools.partial(finish_kernel, count),
        out_shape=(
            jax.ShapeDtypeStruct((rows, width), jnp.float32),
            jax.ShapeDtypeStruct((8, 128), jnp.float32),
        ),
        grid=(4,),
        in_specs=[pl.BlockSpec((nctx * nhead, 128), lambda i: (0, 0)), fin_spec, fin_spec],
        out_specs=(fin_spec, pl.BlockSpec((8, 128), lambda i: (0, 0))),
        scratch_shapes=[pltpu.VMEM((8, 128), jnp.float32)],
        name="finish",
    )(gathered, product, lanczos_vec)
    return next_vec, coef[0, :2]


def solution(mesh):
    placed = (P("ctx", "head"), P(None, "ctx", "head"), P("ctx", "head"), P(), P())
    return jax.shard_map(
        local, mesh=mesh, in_specs=placed, out_specs=(P("ctx", "head"), P()), check_vma=False
    )
```

time: 576 us -> 344 us (0.60)
  blocking collectives: 152 us -> 26.3 us
  matrix products: 72.6 us -> 0 us
  local copies, waits for them, and re-layouts: 74.4 us -> 18.3 us
  Pallas kernels: 0 us -> 43.8 us
  other arithmetic: 36.6 us -> 12.2 us
    psum x1, waiting for transfers between devices: 23.7 us -> 205 us  [from_root(): return lax.psum(block, axis)]
    ppermute x2, waiting for transfers between devices: 180 us -> 0.01 us  [the longest x1 0.01 us: local(): lax.ppermute(own[:, 0], 'ctx', [(i + 1, i) for i in range(nctx - 1)])]
    psum x2 -> x0, blocking collectives: 152 us -> none  [the longest x1 79.1 us: local(): lax.psum(jnp.sum(lanczos_vec * product), ('ctx', 'head')) / entry_count]
    dot_general x8 -> x0, matrix products: 72.6 us -> none  [the longest x2 32.8 us: attend(): jnp.einsum('bqhd,bkhd->bhqk', tangent_out, values, preferred_element_type...]
    pallas_call x0 -> x2, Pallas kernels: none -> 43.8 us  [the longest x1 39.1 us: local(): pl.pallas_call(functools.partial(attention_kernel, nblocks), out_shape=(j...]
    slice x4 -> x2, local copies, waits for them, and re-layouts: 34.9 us -> 1.27 us  [the longest x1 0.68 us: local(): sent = jnp.broadcast_to(stats[:1], (nctx * nhead, 128))]
    all_to_all x0 -> x1, blocking collectives: none -> 26.3 us  [local(): gathered = lax.all_to_all(sent, ('ctx', 'head'), 0, 0, tiled=True)]
    gather x3 -> x1, local copies, waits for them, and re-layouts: 17.9 us -> 6.47 us  [local(): outgoing = jnp.take(own, chosen, axis=1)]
  transfers between devices with their start and end apart: 4 -> 4, of which waited for: 2 -> 1; matrix products, arithmetic and copies ran while one was open for 3% -> 4% of each run, Pallas kernels for 0% -> 0%
where the time goes in v1:
time: 344 us; the launch traced here: 343 us
  waiting for transfers between devices  205 us (60%)
  Pallas kernels  43.8 us (13%)
  blocking collectives  26.3 us (8%)
  between operations  19.4 us (6%)
  local copies, waits for them, and re-layouts  18.3 us (5%)
  starting transfers between devices  17.7 us (5%)
  other arithmetic  12.2 us (4%)
    psum x1, waiting for transfers between devices, from_root(): return lax.psum(block, axis)  205 us
    pallas_call x1, Pallas kernels, local(): pl.pallas_call(functools.partial(attention_kernel, nblocks), out_shape=(j...  39.1 us
    all_to_all x1, blocking collectives, local(): gathered = lax.all_to_all(sent, ('ctx', 'head'), 0, 0, tiled=True)  26.3 us
    all_to_all x1, starting transfers between devices, local(): lax.all_to_all(outgoing, 'ctx', split_axis=1, concat_axis=1, tiled=True)  12.4 us
    all_to_all x1, local copies, waits for them, and re-layouts, local(): lax.all_to_all(outgoing, 'ctx', split_axis=1, concat_axis=1, tiled=True)  7.61 us
    select_n x2, other arithmetic, local(): outgoing = jnp.take(own, chosen, axis=1)  7.48 us
  transfers between devices with their start and end apart: 4, of which 1 were waited for; matrix products, arithmetic and copies ran while one was open for 4% of the time, Pallas kernels for 0%

profile of v1, /device:TPU:1, one launch (start us, length us, event | category | flops | bytes accessed | tf_op | source)
XLA Modules:
  0.0 342.9 jit_solution(17130630142993501962)
XLA Ops:
  7.2 0.7 fusion.2
  7.9 0.1 reduce_sum.15
  8.0 0.1 reduce_sum.20
  8.1 6.5 %gather_fusion = bf16[32,2,128,512]{3,2,1,0:T(8,128)(2,1)} fusion(bf16[2,8,128,512]{3,2,1,0:T(8,128)(2,1)} %bitcast.24, s32[1024]{0:T(1024)S(1)} %pad_clamp_fusion), kind=kCustom, calls=%fused_computation | custom fusion | bytes 16777344 | tf_op jit(solution)/shard_map/jit(_take)/gather | solution.py:184
  14.6 7.5 %select_bitcast_fusion = bf16[2,32,128,512]{3,2,0,1:T(8,128)(2,1)} fusion(bf16[32,2,128,512]{3,2,1,0:T(8,128)(2,1)} %gather_fusion, pred[32]{0:T(512)(128)(4,1)S(1)} %compare_and_fusion), kind=kLoop, calls=%fused_computation.1 | loop fusion | flops 4194304 | bytes 16777248 | tf_op jit(solution)/shard_map/jit(_take)/select_n | solution.py:184
  22.1 12.4 %all-to-all-start = ((bf16[2,32,128,512]{3,2,0,1:T(8,128)(2,1)}), bf16[2,32,128,512]{3,2,0,1:T(8,128)(2,1)}, u32[]{:S(2)}, u32[]{:S(2)}) async-start(bf16[2,32,128,512]{3,2,0,1:T(8,128)(2,1)} %select_bitcast_fusion), calls=%async_computation | async-start | bytes 16777216 | tf_op jit(solution)/shard_map/all_to_all | solution.py:185
  34.6 0.6 fusion.6
  40.4 0.9 dynamic-slice_select_fusion.1
  41.3 1.3 collective-permute-start.1
  42.6 4.0 %collective-permute-start = (bf16[2,128,512]{2,1,0:T(8,128)(2,1)S(1)}, bf16[2,128,512]{2,1,0:T(8,128)(2,1)S(1)}, u32[]{:S(2)}, u32[]{:S(2)}) collective-permute-start(bf16[2,128,512]{2,1,0:T(8,128)(2,1)S(1)} %get-tuple-element.15), channel_id=1, source_target_pairs={{0,8},{8,16},{16,24},{24,32},{32,40},{40,48},{48,56},{56,64},{64,7... | collective-permute-start | bytes 786440 | tf_op jit(solution)/shard_map/ppermute | solution.py:169
  46.6 0.6 add_convert_fusion.edge_ref
  47.2 0.1 copy.9
  47.3 0.1 reshape.41
  47.5 0.5 and_select_fusion.rand_ref
  48.0 205.2 %all-reduce.3.cloned.1.call-done = (bf16[2,1,128,512]{3,2,1,0:T(8,128)(2,1)}, bf16[2,1,128,512]{3,2,1,0:T(8,128)(2,1)}) async-done(((bf16[2,1,128,512]{3,2,1,0:T(8,128)(2,1)}, bf16[2,1,128,512]{3,2,1,0:T(8,128)(2,1)}), (bf16[2,1,128,512]{3,2,1,0:T(8,128)(2,1)}, bf16[2,1,128,512]{3,2,1,0:T(8,128)(2,1)})) %all-reduce.3.cloned.1.call-update) | async-done | bytes 524304 | tf_op jit(solution)/shard_map/psum | solution.py:159
  253.2 1.9 pad_maximum_fusion.glob
  255.0 7.6 %copy.10.rand = bf16[2,32,128,512]{3,2,1,0:T(8,128)(2,1)} copy(bf16[2,32,128,512]{3,2,0,1:T(8,128)(2,1)} %all-to-all-done) | data formatting | bytes 16777216 | tf_op jit(solution)/shard_map/all_to_all | solution.py:185
  262.7 0.7 copy-done.1
  263.4 0.7 copy-done.2
  264.0 39.1 %attend.1 = (f32[1024,512]{1,0:T(8,128)}, f32[8,128]{1,0:T(8,128)}) custom-call(s32[24]{0:T(128)} %and_select_fusion.rand_ref, s32[2]{0:T(128)} %add_convert_fusion.edge_ref, bf16[1024,512]{1,0:T(8,128)(2,1)} %q_ref.1, f32[1024,512]{1,0:T(8,128)} %vec_ref.3, bf16[2,8,128,512]{3,2,1,0:T(8,128)(2,1)} %bitcast.25, bf16[2,128,512]{2,1,0:T(8,128)(2,1)} %copy-done.2, ...), custom_call_target="tpu_custom_call" | custom-call | tf_op jit(solution)/shard_map/attend/pallas_call | solution.py:190
  303.1 0.7 slice_bitcast_fusion.3
  303.9 26.3 %all_to_all.13 = f32[256,1,128]{2,1,0:T(1,128)} all-to-all(f32[256,1,128]{2,1,0:T(1,128)S(1)} %broadcast_in_dim.19), channel_id=1, replica_groups=mesh['ctx'=32,'head'=8] {'ctx','head'}, dimensions={0} | all-to-all | bytes 262144 | tf_op jit(solution)/shard_map/all_to_all | solution.py:211
  330.2 4.7 %finish.1 = (f32[1024,512]{1,0:T(8,128)}, f32[8,128]{1,0:T(8,128)}) custom-call(f32[256,128]{1,0:T(8,128)} %bitcast.27, f32[1024,512]{1,0:T(8,128)} %get-tuple-element.7.prod_ref, f32[1024,512]{1,0:T(8,128)} %vec_ref.3), custom_call_target="tpu_custom_call" | custom-call | tf_op jit(solution)/shard_map/finish/pallas_call | solution.py:215
  334.9 1.2 slice_bitcast_fusion.2
  (17 shorter events, 0.2 us)
Async XLA Ops:
  22.1 12.5 %copy-start.4 = (s32[2]{0:T(128)S(1)}, s32[2]{0:T(128)}, u32[]{:S(2)}) copy-start(s32[2]{0:T(128)} %param.9) | copy-start | bytes 28
  22.1 18.3 %copy-start = (bf16[2,1024,512]{2,1,0:T(8,128)(2,1)S(1)}, bf16[2,1024,512]{2,1,0:T(8,128)(2,1)}, u32[]{:S(2)}) copy-start(bf16[2,1024,512]{2,1,0:T(8,128)(2,1)} %param.6) | copy-start | bytes 6291460
  22.1 25.1 %copy-start.3 = (s32[256,3]{0,1:T(4,128)S(1)}, s32[256,3]{0,1:T(4,128)}, u32[]{:S(2)}) copy-start(s32[256,3]{0,1:T(4,128)} %param.8) | copy-start | bytes 9220
  22.1 233.0 %all-to-all-start = ((bf16[2,32,128,512]{3,2,0,1:T(8,128)(2,1)}), bf16[2,32,128,512]{3,2,0,1:T(8,128)(2,1)}, u32[]{:S(2)}, u32[]{:S(2)}) async-start(bf16[2,32,128,512]{3,2,0,1:T(8,128)(2,1)} %select_bitcast_fusion), calls=%async_computation | async-start | bytes 16777216 | tf_op jit(solution)/shard_map/all_to_all | solution.py:185
  34.5 218.7 %all-reduce.3.cloned.1.call-start = ((), (), s32[]{:S(2)}) async-start(), calls=%async_computation.2 | async-start | bytes 1048576 | tf_op jit(solution)/shard_map/psum | solution.py:159
  41.3 221.4 %collective-permute-start.1 = (bf16[2,128,512]{2,1,0:T(8,128)(2,1)S(1)}, bf16[2,128,512]{2,1,0:T(8,128)(2,1)S(1)}, u32[]{:S(2)}, u32[]{:S(2)}) collective-permute-start(bf16[2,128,512]{2,1,0:T(8,128)(2,1)S(1)} %get-tuple-element.14), channel_id=1, source_target_pairs={{8,0},{16,8},{24,16},{32,24},{40,32},{48,40},{56,48},{64,56},{72,6... | collective-permute-start | bytes 786440 | tf_op jit(solution)/shard_map/ppermute | solution.py:170
  42.6 220.1 %collective-permute-start = (bf16[2,128,512]{2,1,0:T(8,128)(2,1)S(1)}, bf16[2,128,512]{2,1,0:T(8,128)(2,1)S(1)}, u32[]{:S(2)}, u32[]{:S(2)}) collective-permute-start(bf16[2,128,512]{2,1,0:T(8,128)(2,1)S(1)} %get-tuple-element.15), channel_id=1, source_target_pairs={{0,8},{8,16},{16,24},{24,32},{32,40},{40,48},{48,56},{56,64},{64,7... | collective-permute-start | bytes 786440 | tf_op jit(solution)/shard_map/ppermute | solution.py:169
  262.7 0.7 copy-start.1
  263.3 0.7 copy-start.2
Sparse Core Ops, SparseCore 0:
  41.4 211.7 all-reduce.2
